TPU v7x, 32 devices: a whole 2x2x4 slice. The times are simulated.
32 devices in a mesh: dp: 8 (over z, y), tensor: 4 (over x, core).
Axes of the slice: x: 2, y: 2, z: 4, core: 2. Of those that a mesh axis runs over, the one named last changes fastest.
Arguments:
- tokens: int32 [16384], P('dp'), may hold values from 0 to 8190
- lengths: int32 [16, 4], P('dp'), may hold values from 1 to 512, 1024 in all within a row
- timesteps: int32 [16], P('dp'), may hold values from 1 to 1000, as said below
- masks: int32 [16384], P('dp'), may hold values from 0 to 1, as said below
- step_count: int32 [1], replicated, may hold values from 2 to 20
- table: float32 [8192, 768], P('tensor', 'dp'), may hold values from -0.4375 to 0.4375
- joint_weight: float32 [768, 2304], P('dp', 'tensor'), may hold values from -0.21875 to 0.21875
- output_weight: float32 [768, 768], P('tensor', 'dp'), may hold values from -1.75 to 1.75
- upward_weight: float32 [768, 3072], P('dp', 'tensor'), may hold values from -0.21875 to 0.21875
- downward_weight: float32 [3072, 768], P('tensor', 'dp'), may hold values from -0.21875 to 0.21875
- gains: float32 [3, 768], P(None, 'dp'), may hold values from 0.5 to 1.5
- momentum_table: float32 [8192, 768], P('tensor', 'dp'), may hold values from -3.8146973e-06 to 3.8146973e-06
- momentum_joint: float32 [768, 2304], P('dp', 'tensor'), may hold values from -3.8146973e-06 to 3.8146973e-06
- momentum_output: float32 [768, 768], P('tensor', 'dp'), may hold values from -3.8146973e-06 to 3.8146973e-06
- momentum_upward: float32 [768, 3072], P('dp', 'tensor'), may hold values from -3.8146973e-06 to 3.8146973e-06
- momentum_downward: float32 [3072, 768], P('tensor', 'dp'), may hold values from -3.8146973e-06 to 3.8146973e-06
- momentum_gains: float32 [3, 768], P(None, 'dp'), may hold values from -1.9073486e-05 to 1.9073486e-05
- variance_table: float32 [8192, 768], P('tensor', 'dp'), may hold values from 2.9919196e-14 to 1.1967678e-13
- variance_joint: float32 [768, 2304], P('dp', 'tensor'), may hold values from 2.9919196e-14 to 1.1967678e-13
- variance_output: float32 [768, 768], P('tensor', 'dp'), may hold values from 2.9919196e-14 to 1.1967678e-13
- variance_upward: float32 [768, 3072], P('dp', 'tensor'), may hold values from 2.9919196e-14 to 1.1967678e-13
- variance_downward: float32 [3072, 768], P('tensor', 'dp'), may hold values from 2.9919196e-14 to 1.1967678e-13
- variance_gains: float32 [3, 768], P(None, 'dp'), may hold values from 7.4797986e-13 to 2.9919194e-12
Outputs:
- loss: float32 [], replicated
- grad_norm: float32 [], replicated
- new_momentum_table: float32 [8192, 768], P('tensor', 'dp')
- new_variance_table: float32 [8192, 768], P('tensor', 'dp')
- new_table: float32 [8192, 768], P('tensor', 'dp')
- new_momentum_joint: float32 [768, 2304], P('dp', 'tensor')
- new_variance_joint: float32 [768, 2304], P('dp', 'tensor')
- new_joint: float32 [768, 2304], P('dp', 'tensor')
- new_momentum_output: float32 [768, 768], P('tensor', 'dp')
- new_variance_output: float32 [768, 768], P('tensor', 'dp')
- new_output: float32 [768, 768], P('tensor', 'dp')
- new_momentum_upward: float32 [768, 3072], P('dp', 'tensor')
- new_variance_upward: float32 [768, 3072], P('dp', 'tensor')
- new_upward: float32 [768, 3072], P('dp', 'tensor')
- new_momentum_downward: float32 [3072, 768], P('tensor', 'dp')
- new_variance_downward: float32 [3072, 768], P('tensor', 'dp')
- new_downward: float32 [3072, 768], P('tensor', 'dp')
- new_momentum_gains: float32 [3, 768], P(None, 'dp')
- new_variance_gains: float32 [3, 768], P(None, 'dp')
- new_gains: float32 [3, 768], P(None, 'dp')
Inputs may be any that keep to these rules, and one draw needn't show every extreme that they name: `timesteps`: a sequence's timestep is drawn uniformly; some sequence has timestep 1 and some has 1000. `masks`: each position of sequence s is masked independently with probability timesteps[s] / 1000.
All inputs are finite; a program needn't handle non-finite values.
Results may differ from a plain program's by a relative error of at most 0.0082.
Values may be sent and summed in bfloat16 or wider, within the bound.
A program may use at most 192 MiB of HBM per device.

v0:
```python
import jax
import jax.numpy as jnp
from jax import lax
from jax.sharding import PartitionSpec as P

D = 768
HEAD_DIM = 64
VOCAB = 8192
SEQ_LEN = 1024
DOCS = 4
T_DIFF = 1000
eps_norm = 1e-06
neg_fill = -1000000000.0
beta_one = 0.9
beta_two = 0.999
adam_eps = 1e-08
clip_at = 0.02
rates = (0.05, 0.03, 0.25, 0.03, 0.03, 0.3)
decays = (0.1, 0.1, 0.1, 0.1, 0.1, 0.0)


def joined(value, axis, join):
    pieces = jax.tree.map(lambda part: lax.all_gather(part, axis), value)
    head = jax.tree.map(lambda part: part[0], pieces)
    tail = jax.tree.map(lambda part: part[1:], pieces)
    running, _ = lax.scan(lambda running, piece: (join(running, piece), None), head, tail)
    return running


def tensor_total(partial_value):
    return lax.psum(partial_value, "tensor")


def norm_apply(values, gain):
    inverse = lax.rsqrt(jnp.mean(values * values, axis=-1, keepdims=True) + eps_norm)
    return values * inverse * gain


def norm_back(values, gain, upstream):
    inverse = lax.rsqrt(jnp.mean(values * values, axis=-1, keepdims=True) + eps_norm)
    gain_grad = jnp.sum(upstream * values * inverse, axis=0)
    scaled = upstream * gain
    inner = jnp.mean(scaled * values, axis=-1, keepdims=True)
    return (inverse * (scaled - values * inverse * inverse * inner), gain_grad)


def rotate(values, cosine, sine):
    middle = values.shape[-1] // 2
    front_part = values[..., :middle]
    back_part = values[..., middle:]
    return jnp.concatenate(
        [front_part * cosine - back_part * sine, back_part * cosine + front_part * sine], axis=-1
    )


def gelu_exact(values):
    return jax.nn.gelu(values, approximate=False)


def packing(lengths, tokens, masks, timesteps):
    seq_count = lengths.shape[0]
    position = jnp.arange(SEQ_LEN, dtype=jnp.int32)
    doc_ends = jnp.cumsum(lengths, axis=1)
    doc_starts = doc_ends - lengths
    segment = jnp.sum((position[None, :, None] >= doc_ends[:, None, :]).astype(jnp.int32), axis=2)
    chosen = segment[:, :, None] == jnp.arange(DOCS, dtype=jnp.int32)[None, None, :]
    offset = position[None, :] - jnp.sum(jnp.where(chosen, doc_starts[:, None, :], 0), axis=2)
    is_real = segment < DOCS - 1
    targets = tokens.reshape(seq_count, SEQ_LEN)
    corrupt = masks.reshape(seq_count, SEQ_LEN) == 1
    inputs = jnp.where(corrupt, VOCAB - 1, targets)
    factor = jnp.where(timesteps == 1, 1.0, T_DIFF / timesteps.astype(jnp.float32))
    weights = jnp.where(corrupt & is_real, factor[:, None], 0.0)
    inverse_freq = 10000.0 ** (-jnp.arange(HEAD_DIM // 2, dtype=jnp.float32) / (HEAD_DIM // 2))
    angles = offset.astype(jnp.float32)[:, :, None] * inverse_freq
    return (inputs, targets, weights, segment, is_real, jnp.cos(angles), jnp.sin(angles))


def scores_of(query, key_rows, segment):
    same_doc = segment[:, None] == segment[None, :]
    scores = jnp.einsum(
        "qhe,khe->hqk", query, key_rows, preferred_element_type=jnp.float32
    ) * HEAD_DIM ** (-0.5)
    return jnp.where(same_doc[None], scores, neg_fill)


def attend_one(query, key_rows, value_rows, segment):
    scores = scores_of(query, key_rows, segment)
    row_max = jnp.max(scores, axis=-1, keepdims=True)
    expd = jnp.exp(scores - row_max)
    summed = jnp.sum(expd, axis=-1, keepdims=True)
    probs = (expd / summed).astype(jnp.bfloat16)
    output = jnp.einsum("hqk,khe->qhe", probs, value_rows, preferred_element_type=jnp.float32)
    return (output.astype(jnp.bfloat16), (row_max + jnp.log(summed))[..., 0])


def attend_back(query, key_rows, value_rows, segment, row_lse, grad_out):
    scores = scores_of(query, key_rows, segment)
    probs = jnp.exp(scores - row_lse[..., None])
    value_grad = jnp.einsum(
        "hqk,qhe->khe", probs.astype(jnp.bfloat16), grad_out, preferred_element_type=jnp.float32
    )
    prob_grad = jnp.einsum("qhe,khe->hqk", grad_out, value_rows, preferred_element_type=jnp.float32)
    inner = jnp.sum(prob_grad * probs, axis=-1, keepdims=True)
    score_grad = (probs * (prob_grad - inner)).astype(jnp.bfloat16)
    query_grad = jnp.einsum(
        "hqk,khe->qhe", score_grad, key_rows, preferred_element_type=jnp.float32
    ) * HEAD_DIM ** (-0.5)
    key_grad = jnp.einsum(
        "hqk,qhe->khe", score_grad, query, preferred_element_type=jnp.float32
    ) * HEAD_DIM ** (-0.5)
    return (query_grad, key_grad, value_grad)


def vocab_stats(normed, vocab_rows, targets, vocab_start):
    logits = jnp.einsum("rd,vd->rv", normed, vocab_rows, preferred_element_type=jnp.float32)
    local_max = jnp.max(logits, axis=-1)
    local_sum = jnp.sum(jnp.exp(logits - local_max[:, None]), axis=-1)
    target_hit = (targets - vocab_start)[:, None] == jnp.arange(
        vocab_rows.shape[0], dtype=jnp.int32
    )[None, :]
    return (local_max, local_sum, jnp.sum(jnp.where(target_hit, logits, 0.0), axis=-1))


def vocab_back(normed, vocab_rows, targets, vocab_start, row_lse, row_weight):
    logits = jnp.einsum("rd,vd->rv", normed, vocab_rows, preferred_element_type=jnp.float32)
    target_hit = (
        (targets - vocab_start)[:, None]
        == jnp.arange(vocab_rows.shape[0], dtype=jnp.int32)[None, :]
    ).astype(jnp.float32)
    logit_grad = (row_weight[:, None] * (jnp.exp(logits - row_lse[:, None]) - target_hit)).astype(
        jnp.bfloat16
    )
    table_part = jnp.einsum("rv,rd->vd", logit_grad, normed, preferred_element_type=jnp.float32)
    normed_grad = jnp.einsum(
        "rv,vd->rd", logit_grad, vocab_rows, preferred_element_type=jnp.float32
    )
    return (table_part, normed_grad)


def combine(earlier, later):
    max_early, sum_early, pick_early = earlier
    max_late, sum_late, pick_late = later
    top_value = jnp.maximum(max_early, max_late)
    return (
        top_value,
        sum_early * jnp.exp(max_early - top_value) + sum_late * jnp.exp(max_late - top_value),
        pick_early + pick_late,
    )


def per_device(
    tokens,
    lengths,
    timesteps,
    masks,
    step_count,
    table,
    joint_weight,
    output_weight,
    upward_weight,
    downward_weight,
    gains,
    momentum_table,
    momentum_joint,
    momentum_output,
    momentum_upward,
    momentum_downward,
    momentum_gains,
    variance_table,
    variance_joint,
    variance_output,
    variance_upward,
    variance_downward,
    variance_gains,
):
    vocab_rows, joint_rows, output_rows, upward_rows, downward_rows, gain_rows = (
        lax.all_gather(table.astype(jnp.bfloat16), "dp", axis=1, tiled=True),
        lax.all_gather(joint_weight.astype(jnp.bfloat16), "dp", axis=0, tiled=True),
        lax.all_gather(output_weight.astype(jnp.bfloat16), "dp", axis=1, tiled=True),
        lax.all_gather(upward_weight.astype(jnp.bfloat16), "dp", axis=0, tiled=True),
        lax.all_gather(downward_weight.astype(jnp.bfloat16), "dp", axis=1, tiled=True),
        lax.all_gather(gains.astype(jnp.bfloat16), "dp", axis=1, tiled=True),
    )
    gain_full = gain_rows.astype(jnp.float32)
    inputs, targets, weights, segment, is_real, cosine, sine = packing(
        lengths, tokens, masks, timesteps
    )
    seq_count = lengths.shape[0]
    row_count = tokens.shape[0]
    vocab_local = vocab_rows.shape[0]
    vocab_start = lax.axis_index("tensor") * vocab_local
    local_ids = inputs.reshape(row_count) - vocab_start
    inside = (local_ids >= 0) & (local_ids < vocab_local)
    safe_ids = jnp.clip(local_ids, 0, vocab_local - 1)
    looked = jnp.take(vocab_rows, safe_ids, axis=0).astype(jnp.float32) * D**0.5
    embedded = tensor_total(jnp.where(inside[:, None], looked, 0.0))
    normed_one = norm_apply(embedded, gain_full[0]).astype(jnp.bfloat16)
    heads_local = joint_rows.shape[1] // (3 * HEAD_DIM)
    projected = jnp.dot(normed_one, joint_rows, preferred_element_type=jnp.float32).reshape(
        seq_count, SEQ_LEN, heads_local, 3, HEAD_DIM
    )
    rot_cos = cosine[:, :, None, :]
    rot_sin = sine[:, :, None, :]
    query = rotate(projected[:, :, :, 0], rot_cos, rot_sin).astype(jnp.bfloat16)
    key_rows = rotate(projected[:, :, :, 1], rot_cos, rot_sin).astype(jnp.bfloat16)
    value_rows = projected[:, :, :, 2].astype(jnp.bfloat16)
    attended, attn_lse = lax.map(
        lambda items: attend_one(*items), (query, key_rows, value_rows, segment)
    )
    attended_flat = attended.reshape(row_count, heads_local * HEAD_DIM)
    attn_part = jnp.dot(attended_flat, output_rows, preferred_element_type=jnp.float32)
    after_attn = embedded + tensor_total(attn_part)
    normed_two = norm_apply(after_attn, gain_full[1]).astype(jnp.bfloat16)
    pre_gelu = jnp.dot(normed_two, upward_rows, preferred_element_type=jnp.float32)
    gelu_value, gelu_pull = jax.vjp(gelu_exact, pre_gelu)
    activated = gelu_value.astype(jnp.bfloat16)
    mlp_part = jnp.dot(activated, downward_rows, preferred_element_type=jnp.float32)
    after_mlp = after_attn + tensor_total(mlp_part)
    normed_out = norm_apply(after_mlp, gain_full[2]).astype(jnp.bfloat16)
    per_seq = normed_out.reshape(seq_count, SEQ_LEN, D)
    stats = lax.map(
        lambda items: vocab_stats(items[0], vocab_rows, items[1], vocab_start), (per_seq, targets)
    )
    row_max, row_sum, row_pick = joined(
        (stats[0].reshape(row_count), stats[1].reshape(row_count), stats[2].reshape(row_count)),
        "tensor",
        combine,
    )
    row_lse = row_max + jnp.log(row_sum)
    loss_local = jnp.sum(weights.reshape(row_count) * (row_lse - row_pick))
    count_local = jnp.sum(is_real.astype(jnp.float32))
    loss_total, count_total = lax.psum((loss_local, count_local), "dp")

    def head_step(carry, items):
        normed_rows, target_rows, lse_rows, weight_rows = items
        table_part, normed_grad = vocab_back(
            normed_rows, vocab_rows, target_rows, vocab_start, lse_rows, weight_rows
        )
        return (carry + table_part, normed_grad)

    table_grad, out_grad = lax.scan(
        head_step,
        jnp.zeros(vocab_rows.shape, jnp.float32),
        (per_seq, targets, row_lse.reshape(seq_count, SEQ_LEN), weights),
    )
    out_grad = tensor_total(out_grad.reshape(row_count, D))
    mlp_grad, gain_three = norm_back(after_mlp, gain_full[2], out_grad)
    mlp_branch = mlp_grad.astype(jnp.bfloat16)
    downward_grad = jnp.einsum(
        "rf,rd->fd", activated, mlp_branch, preferred_element_type=jnp.float32
    )
    act_grad = jnp.einsum(
        "rd,fd->rf", mlp_branch, downward_rows, preferred_element_type=jnp.float32
    )
    up_input = gelu_pull(act_grad)[0].astype(jnp.bfloat16)
    upward_grad = jnp.einsum("rd,rf->df", normed_two, up_input, preferred_element_type=jnp.float32)
    normed_two_grad = tensor_total(
        jnp.einsum("rf,df->rd", up_input, upward_rows, preferred_element_type=jnp.float32)
    )
    attn_in_grad, gain_two = norm_back(after_attn, gain_full[1], normed_two_grad)
    resid_one = mlp_grad + attn_in_grad
    attn_branch = resid_one.astype(jnp.bfloat16)
    output_grad = jnp.einsum(
        "ra,rd->ad", attended_flat, attn_branch, preferred_element_type=jnp.float32
    )
    attended_grad = (
        jnp.einsum("rd,ad->ra", attn_branch, output_rows, preferred_element_type=jnp.float32)
        .astype(jnp.bfloat16)
        .reshape(seq_count, SEQ_LEN, heads_local, HEAD_DIM)
    )
    query_grad, key_grad, value_grad = lax.map(
        lambda items: attend_back(*items),
        (query, key_rows, value_rows, segment, attn_lse, attended_grad),
    )
    query_grad = rotate(query_grad, rot_cos, -rot_sin)
    key_grad = rotate(key_grad, rot_cos, -rot_sin)
    proj_grad = (
        jnp.stack([query_grad, key_grad, value_grad], axis=3)
        .reshape(row_count, heads_local * 3 * HEAD_DIM)
        .astype(jnp.bfloat16)
    )
    joint_grad = jnp.einsum("rd,rc->dc", normed_one, proj_grad, preferred_element_type=jnp.float32)
    normed_one_grad = tensor_total(
        jnp.einsum("rc,dc->rd", proj_grad, joint_rows, preferred_element_type=jnp.float32)
    )
    embed_in, gain_one = norm_back(embedded, gain_full[0], normed_one_grad)
    embed_grad = resid_one + embed_in
    gain_grad = jnp.stack([gain_one, gain_two, gain_three])
    table_grad = table_grad + jax.ops.segment_sum(
        jnp.where(inside[:, None], embed_grad * D**0.5, 0.0), safe_ids, num_segments=vocab_local
    )
    table_sum, joint_sum, output_sum, upward_sum, downward_sum, gain_sum = (
        lax.psum_scatter(table_grad, "dp", scatter_dimension=1, tiled=True),
        lax.psum_scatter(joint_grad, "dp", scatter_dimension=0, tiled=True),
        lax.psum_scatter(output_grad, "dp", scatter_dimension=1, tiled=True),
        lax.psum_scatter(upward_grad, "dp", scatter_dimension=0, tiled=True),
        lax.psum_scatter(downward_grad, "dp", scatter_dimension=1, tiled=True),
        lax.psum_scatter(gain_grad, "dp", scatter_dimension=1, tiled=True),
    )
    reduced = (table_sum, joint_sum, output_sum, upward_sum, downward_sum, gain_sum)
    local_square = jnp.zeros((), jnp.float32)
    for grad_item in reduced[:5]:
        local_square = local_square + jnp.sum(grad_item * grad_item)
    local_square = local_square + jnp.sum(gain_sum * gain_sum) / lax.axis_size("tensor")
    square_total = lax.psum(local_square, ("dp", "tensor"))
    grad_norm = jnp.sqrt(square_total) / count_total
    clip_scale = jnp.minimum(1.0, clip_at / grad_norm)
    loss = loss_total / count_total
    step_float = step_count[0].astype(jnp.float32)
    fix_one = 1.0 - jnp.power(beta_one, step_float)
    fix_two = 1.0 - jnp.power(beta_two, step_float)
    masters = (table, joint_weight, output_weight, upward_weight, downward_weight, gains)
    moments_one = (
        momentum_table,
        momentum_joint,
        momentum_output,
        momentum_upward,
        momentum_downward,
        momentum_gains,
    )
    moments_two = (
        variance_table,
        variance_joint,
        variance_output,
        variance_upward,
        variance_downward,
        variance_gains,
    )
    updated = []
    for index in range(6):
        clipped = reduced[index] / count_total * clip_scale
        moment_one = beta_one * moments_one[index] + (1.0 - beta_one) * clipped
        moment_two = beta_two * moments_two[index] + (1.0 - beta_two) * clipped * clipped
        stepped = moment_one / fix_one / (jnp.sqrt(moment_two / fix_two) + adam_eps)
        master = masters[index]
        updated.extend(
            [moment_one, moment_two, master - rates[index] * (stepped + decays[index] * master)]
        )
    return tuple([loss, grad_norm] + updated)


def solution(mesh):
    placed = (
        P("dp"),
        P("dp", None),
        P("dp"),
        P("dp"),
        P(),
        P("tensor", "dp"),
        P("dp", "tensor"),
        P("tensor", "dp"),
        P("dp", "tensor"),
        P("tensor", "dp"),
        P(None, "dp"),
        P("tensor", "dp"),
        P("dp", "tensor"),
        P("tensor", "dp"),
        P("dp", "tensor"),
        P("tensor", "dp"),
        P(None, "dp"),
        P("tensor", "dp"),
        P("dp", "tensor"),
        P("tensor", "dp"),
        P("dp", "tensor"),
        P("tensor", "dp"),
        P(None, "dp"),
    )
    return jax.shard_map(
        per_device,
        mesh=mesh,
        in_specs=placed,
        out_specs=(
            P(),
            P(),
            P("tensor", "dp"),
            P("tensor", "dp"),
            P("tensor", "dp"),
            P("dp", "tensor"),
            P("dp", "tensor"),
            P("dp", "tensor"),
            P("tensor", "dp"),
            P("tensor", "dp"),
            P("tensor", "dp"),
            P("dp", "tensor"),
            P("dp", "tensor"),
            P("dp", "tensor"),
            P("tensor", "dp"),
            P("tensor", "dp"),
            P("tensor", "dp"),
            P(None, "dp"),
            P(None, "dp"),
            P(None, "dp"),
        ),
        check_vma=False,
    )
```

profile of v0, /device:TPU:0, one launch (start us, length us, event | category | flops | bytes accessed | tf_op | source)
XLA Modules:
  0.0 1683.7 jit_solution(2242139781662490906)
XLA Ops:
  11.9 62.1 %all-gather.8.cloned.1.call-done = bf16[2048,768]{0,1:T(8,128)(2,1)} async-done(((bf16[2048,96]{0,1:T(8,128)(2,1)}), bf16[2048,768]{0,1:T(8,128)(2,1)}) %all-gather.8.cloned.1.call-update) | async-done | bytes 3145744 | tf_op jit(solution)/shard_map/all_gather | solution.py:178
  77.2 9.6 gather_fusion
  86.8 4.6 multiply_select_fusion.1
  91.7 18.2 %all-gather = bf16[8,96,3]{1,2,0:T(4,128)(2,1)S(1)} all-gather(bf16[1,96,3]{1,2,0:T(4,128)(2,1)S(1)} %convert_bitcast_fusion.1), channel_id=1, replica_groups=mesh['dp'=8,'tensor'=4] {'dp'}, dimensions={0}, use_global_device_ids=true | all-gather | bytes 5184 | tf_op jit(solution)/shard_map/all_gather | solution.py:183
  111.0 33.3 %all_gather.30 = bf16[192,768]{0,1:T(8,128)(2,1)} all-gather(bf16[192,96]{0,1:T(8,128)(2,1)S(1)} %copy.126), channel_id=1, replica_groups=mesh['dp'=8,'tensor'=4] {'dp'}, dimensions={1}, use_global_device_ids=true | all-gather | bytes 331776 | tf_op jit(solution)/shard_map/all_gather | solution.py:180
  146.0 32.9 %all_gather.29 = bf16[768,576]{1,0:T(8,128)(2,1)S(1)} all-gather(bf16[96,576]{1,0:T(8,128)(2,1)S(1)} %convert_element_type.106), channel_id=1, replica_groups=mesh['dp'=8,'tensor'=4] {'dp'}, dimensions={0}, use_global_device_ids=true | all-gather | bytes 995328 | tf_op jit(solution)/shard_map/all_gather | solution.py:179
  178.9 30.9 %all-reduce.8.cloned.1.call-done = f32[2048,768]{1,0:T(8,128)} async-done(((f32[2048,768]{1,0:T(8,128)}), f32[2048,768]{1,0:T(8,128)}) %all-reduce.8.cloned.1.call-update) | async-done | bytes 6291472 | tf_op jit(solution)/shard_map/psum | solution.py:31
  214.4 4.5 fusion.113
  218.9 7.5 reshape.255
  236.0 29.3 %while.72 = (s32[]{:T(128)}, bf16[2,1024,3,64]{1,3,2,0:T(8,128)(2,1)}, f32[2,3,1024]{2,1,0:T(4,128)S(1)}, bf16[2,1024,3,64]{1,3,2,0:T(8,128)(2,1)}, s32[2,1024]{...) while((s32[]{:T(128)}, ...), condition=%wide.region_8.9_spmd.clone, body=%wide.region_5.8_spmd.sunk.clone | while | flops 844297216 | bytes 47835256 | solution.py:208
  236.7 4.2 fusion.200
  240.9 3.9 fusion.201
  244.8 5.7 fusion.202
  251.2 4.2 fusion.200
  255.5 3.9 fusion.201
  259.3 5.7 fusion.202
  273.8 118.2 %all-reduce.10.cloned.1.call-done = f32[2048,768]{1,0:T(8,128)} async-done(((f32[2048,768]{1,0:T(8,128)}), f32[2048,768]{1,0:T(8,128)}) %all-reduce.10.cloned.1.call-update) | async-done | bytes 6291472 | tf_op jit(solution)/shard_map/psum | solution.py:31
  392.0 7.9 multiply_reduce_fusion.8
  400.0 36.0 %all-gather.10.cloned.1.call-done = bf16[768,768]{1,0:T(8,128)(2,1)} async-done(((bf16[96,768]{1,0:T(8,128)(2,1)}), bf16[768,768]{1,0:T(8,128)(2,1)}) %all-gather.10.cloned.1.call-update) | async-done | bytes 1179664 | tf_op jit(solution)/shard_map/all_gather | solution.py:181
  435.9 19.1 %multiply_convert_fusion.3 = (bf16[2048,768]{1,0:T(8,128)(2,1)S(1)}, f32[2048,768]{1,0:T(8,128)}, f32[2048,768]{1,0:T(8,128)}) fusion(bf16[768,768]{1,0:T(8,128)(2,1)} %all-gather.10.cloned.1.call-done, f32[2048,768]{1,0:T(8,128)} %get-tuple-element.571, f32[768]{0:T(1024)S(1)} %copy-done.60, f32[2048]{0:T(1024)S(1)} %add_rsqrt_fusion.1), kind=kOutput, calls=%fused_computation.111 | convolution fusion | flops 2522873856 | bytes 23211008 | tf_op jit(solution)/shard_map/dot_general | solution.py:215
  455.1 23.3 %all-gather.12.cloned.1.call-done = bf16[768,768]{0,1:T(8,128)(2,1)} async-done(((bf16[768,96]{0,1:T(8,128)(2,1)}), bf16[768,768]{0,1:T(8,128)(2,1)}) %all-gather.12.cloned.1.call-update) | async-done | bytes 1179664 | tf_op jit(solution)/shard_map/all_gather | solution.py:182
  478.4 5.8 fusion.125
  485.1 117.6 %all-reduce.12.cloned.1.call-done = f32[2048,768]{1,0:T(8,128)} async-done(((f32[2048,768]{1,0:T(8,128)}), f32[2048,768]{1,0:T(8,128)}) %all-reduce.12.cloned.1.call-update) | async-done | bytes 6291472 | tf_op jit(solution)/shard_map/psum | solution.py:31
  602.7 5.4 multiply_reduce_fusion.7
  613.7 16.7 while.73
  613.7 4.9 fusion.204
  622.1 4.9 fusion.204
  630.4 5.2 all-gather.2
  635.6 5.2 all-gather.1
  640.9 5.2 all-gather.3
  647.4 34.1 %while.76 = (s32[]{:T(128)}, f32[2048,768]{1,0:T(8,128)}, f32[2,1024,768]{2,1,0:T(8,128)}, f32[2,1024]{1,0:T(2,128)S(1)}, bf16[2,1024,768]{2,1,0:T(8,128)(2,1)},...) while((s32[]{:T(128)}, f32[2048,768]{1,0:T(8,128)}, ...), condition=%wide.region_25.26_spmd.clone.clone, body=%wide.region_24.25_spmd.clone.sunk.clone | while | flops 9679406080 | bytes 151032080 | solution.py:242
  647.5 5.7 multiply_convert_fusion.15
  653.2 5.1 select_add_fusion.3
  664.5 5.7 multiply_convert_fusion.15
  670.2 5.1 select_add_fusion.3
  681.6 119.9 %all-reduce.14.cloned.1.call-done = f32[2048,768]{1,0:T(8,128)} async-done(((f32[2048,768]{1,0:T(8,128)}), f32[2048,768]{1,0:T(8,128)}) %all-reduce.14.cloned.1.call-update) | async-done | bytes 6291472 | tf_op jit(solution)/shard_map/psum | solution.py:31
  801.5 6.3 multiply_reduce_fusion.1
  807.9 3.8 subtract_multiply_fusion
  812.2 8.1 add_convert_fusion
  822.0 4.5 fusion.126
  826.7 119.9 %all-reduce.16.cloned.1.call-done = f32[2048,768]{1,0:T(8,128)} async-done(((f32[2048,768]{1,0:T(8,128)}), f32[2048,768]{1,0:T(8,128)}) %all-reduce.16.cloned.1.call-update) | async-done | bytes 6291472 | tf_op jit(solution)/shard_map/psum | solution.py:31
  946.6 6.1 multiply_reduce_fusion.2
  953.0 5.6 multiply_add_fusion.1
  965.4 50.7 %while.75 = (s32[]{:T(128)}, f32[2,1024,3,64]{1,3,2,0:T(8,128)}, f32[2,1024,3,64]{1,3,2,0:T(8,128)}, bf16[2,1024,3,64]{1,3,2,0:T(8,128)(2,1)}, bf16[2,1024,3,64]...) while((s32[]{:T(128)}, f32[2,1024,3,64]{1,3,2,0:T(8,128)}, ...), condition=%wide.region_32.33_spmd.clone, body=%wide.region_30.32_spmd.sunk.clone | while | flops 2061890560 | bytes 135247168 | solution.py:272
  971.9 7.1 multiply_reduce_fusion.18
  979.1 7.1 multiply_convert_fusion.14
  996.9 7.1 multiply_reduce_fusion.18
  1004.1 7.1 multiply_convert_fusion.14
  1022.2 4.7 fusion.127
  1028.0 5.0 fusion.95
  1033.1 8.1 fusion.89
  1041.5 8.0 fusion.110
  1049.5 97.3 %all-reduce.18.cloned.1.call-done = f32[2048,768]{1,0:T(8,128)} async-done(((f32[2048,768]{1,0:T(8,128)}), f32[2048,768]{1,0:T(8,128)}) %all-reduce.18.cloned.1.call-update) | async-done | bytes 6291472 | tf_op jit(solution)/shard_map/psum | solution.py:31
  1146.8 5.4 multiply_reduce_fusion.3
  1153.3 7.1 fusion.112
  1160.4 23.7 %scatter_custom_fusion = f32[2048,768]{1,0:T(8,128)} fusion(f32[2048,768]{1,0:T(8,128)} %get-tuple-element.250, s32[2048]{0:T(1024)} %copy-done.65, f32[2048,768]{1,0:T(8,128)} %copy-done.5, f32[2048,768]{1,0:T(8,128)} %all-reduce.18.cloned.1.call-done, f32[2048,768]{1,0:T(8,128)} %all-reduce.8.cloned.1.call-done, f32[2048]{0:T(1024)S(1)} %broadcast_multiply_fusion, ...), kind=kCustom, calls=%fused_computation.95 | custom fusion | flops 15728640 | bytes 25188352 | tf_op jit(solution)/shard_map/scatter-add | solution.py:290
  1184.2 6.6 copy.136
  1192.3 21.7 %all-reduce = (f32[]{:T(128)}, f32[]{:T(128)}) all-reduce(f32[]{:T(128)} %get-tuple-element.564, f32[]{:T(128)} %convert_reduce_fusion.1), channel_id=1, replica_groups=mesh['dp'=8,'tensor'=4] {'dp'}, use_global_device_ids=true, to_apply=%region_21.22 | all-reduce | flops 2 | bytes 16 | tf_op jit(solution)/shard_map/psum | solution.py:233
  1216.4 68.9 %reduce-scatter.17.cloned.1.call-done = f32[768,96]{0,1:T(8,128)} async-done(((f32[768,768]{0,1:T(8,128)}), f32[768,96]{0,1:T(8,128)}) %reduce-scatter.17.cloned.1.call-update) | async-done | bytes 294928 | tf_op jit(solution)/shard_map/reduce_scatter | solution.py:298
  1287.0 70.1 %reduce-scatter.15.cloned.1.call-done = f32[96,768]{1,0:T(8,128)} async-done(((f32[768,768]{1,0:T(8,128)}), f32[96,768]{1,0:T(8,128)}) %reduce-scatter.15.cloned.1.call-update) | async-done | bytes 294928 | tf_op jit(solution)/shard_map/reduce_scatter | solution.py:297
  1358.7 63.0 %reduce-scatter.23.cloned.1.call-done = f32[96,3]{1,0:T(8,128)} async-done(((f32[768,3]{1,0:T(8,128)}), f32[96,3]{1,0:T(8,128)}) %reduce-scatter.23.cloned.1.call-update) | async-done | bytes 1168
  1423.8 67.5 %reduce-scatter.13.cloned.1.call-done = f32[96,576]{1,0:T(8,128)} async-done(((f32[768,576]{1,0:T(8,128)}), f32[96,576]{1,0:T(8,128)}) %reduce-scatter.13.cloned.1.call-update) | async-done | bytes 221200 | tf_op jit(solution)/shard_map/reduce_scatter | solution.py:295
  1492.9 118.5 %reduce-scatter.19.cloned.1.call-done = f32[96,2048]{1,0:T(8,128)} async-done(((f32[768,2048]{1,0:T(8,128)}), f32[96,2048]{1,0:T(8,128)}) %reduce-scatter.19.cloned.1.call-update) | async-done | bytes 786448
  1618.5 39.6 %psum.71 = f32[]{:T(128)} all-reduce(f32[]{:T(128)S(6)} %add.255), channel_id=1, replica_groups=mesh['dp'=8,'tensor'=4] {'dp','tensor'}, use_global_device_ids=true, to_apply=%region_51.52 | all-reduce | flops 1 | bytes 8 | tf_op jit(solution)/shard_map/psum | solution.py:306
  (370 shorter events, 127.3 us)
Async XLA Ops:
  7.2 66.8 %all-gather.8.cloned.1.call-start = ((), (), s32[]{:S(2)}) async-start(), calls=%async_computation.6 | async-start | bytes 3538944 | tf_op jit(solution)/shard_map/all_gather | solution.py:178
  9.2 200.6 %all-reduce.8.cloned.1.call-start = ((), (), s32[]{:S(2)}) async-start(), calls=%async_computation.7 | async-start | bytes 12582912 | tf_op jit(solution)/shard_map/psum | solution.py:31
  10.0 76.8 %copy-start.68 = (pred[2048]{0:T(1024)(128)(4,1)}, pred[2048]{0:T(1024)(128)(4,1)S(1)}, u32[]{:S(2)}) copy-start(pred[2048]{0:T(1024)(128)(4,1)S(1)} %get-tuple-element.572) | copy-start | bytes 6148
  77.2 9.6 copy-start
  86.8 23.2 %copy-start.45 = (f32[192,96]{1,0:T(8,128)S(1)}, f32[192,96]{1,0:T(8,128)}, u32[]{:S(2)}) copy-start(f32[192,96]{1,0:T(8,128)} %param.40) | copy-start | bytes 221188
  86.8 23.3 %copy-start.36 = (f32[96,576]{1,0:T(8,128)S(1)}, f32[96,576]{1,0:T(8,128)}, u32[]{:S(2)}) copy-start(f32[96,576]{1,0:T(8,128)} %param.39) | copy-start | bytes 663556
  91.4 300.6 %all-reduce.10.cloned.1.call-start = ((), (), s32[]{:S(2)}) async-start(), calls=%async_computation.8 | async-start | bytes 12582912 | tf_op jit(solution)/shard_map/psum | solution.py:31
  110.9 108.1 %copy-start.52 = (f32[768]{0:T(1024)}, f32[768]{0:T(1024)S(1)}, u32[]{:S(2)}) copy-start(f32[768]{0:T(1024)S(1)} %get-tuple-element.457) | copy-start | bytes 9220
  146.0 87.5 %copy-start.25 = (f32[2,1024,32]{1,2,0:T(8,128)}, f32[2,1024,32]{1,2,0:T(8,128)S(1)}, u32[]{:S(2)}) copy-start(f32[2,1024,32]{1,2,0:T(8,128)S(1)} %get-tuple-element.602) | copy-start | bytes 786436
  178.9 40.0 %copy-start.18 = (bf16[768,576]{1,0:T(8,128)(2,1)}, bf16[768,576]{1,0:T(8,128)(2,1)S(1)}, u32[]{:S(2)}) copy-start(bf16[768,576]{1,0:T(8,128)(2,1)S(1)} %all_gather.29) | copy-start | bytes 2654212
  213.2 5.7 copy-start.46
  236.0 32.4 %copy-start.20 = (bf16[192,768]{0,1:T(8,128)(2,1)S(1)}, bf16[192,768]{0,1:T(8,128)(2,1)}, u32[]{:S(2)}) copy-start(bf16[192,768]{0,1:T(8,128)(2,1)} %all_gather.30) | copy-start | bytes 884740
  265.3 6.8 copy-start.48
  265.3 219.7 %copy-start.43 = (s32[2,1024]{1,0:T(2,128)}, s32[2,1024]{1,0:T(2,128)S(1)}, u32[]{:S(2)}) copy-start(s32[2,1024]{1,0:T(2,128)S(1)} %get-tuple-element.1178) | copy-start | bytes 24580
  272.1 163.9 %all-gather.10.cloned.1.call-start = ((), (), s32[]{:S(2)}) async-start(), calls=%async_computation.9 | async-start | bytes 1327104 | tf_op jit(solution)/shard_map/all_gather | solution.py:181
  272.8 205.6 %all-gather.12.cloned.1.call-start = ((), (), s32[]{:S(2)}) async-start(), calls=%async_computation.10 | async-start | bytes 1327104 | tf_op jit(solution)/shard_map/all_gather | solution.py:182
  273.7 162.2 %copy-start.60 = (f32[768]{0:T(1024)S(1)}, f32[768]{0:T(1024)}, u32[]{:S(2)}) copy-start(f32[768]{0:T(1024)} %get-tuple-element.456) | copy-start | bytes 9220
  273.7 329.0 %all-reduce.12.cloned.1.call-start = ((), (), s32[]{:S(2)}) async-start(), calls=%async_computation.11 | async-start | bytes 12582912 | tf_op jit(solution)/shard_map/psum | solution.py:31
  399.9 55.1 %copy-start.55 = (f32[2048]{0:T(1024)}, f32[2048]{0:T(1024)S(1)}, u32[]{:S(2)}) copy-start(f32[2048]{0:T(1024)S(1)} %add_rsqrt_fusion.1) | copy-start | bytes 24580
  455.1 29.1 %copy-start.81 = (bf16[2048,768]{1,0:T(8,128)(2,1)}, bf16[2048,768]{1,0:T(8,128)(2,1)S(1)}, u32[]{:S(2)}) copy-start(bf16[2048,768]{1,0:T(8,128)(2,1)S(1)} %get-tuple-element.568) | copy-start | bytes 9437188
  484.2 317.2 %all-reduce.14.cloned.1.call-start = ((), (), s32[]{:S(2)}) async-start(), calls=%async_computation.12 | async-start | bytes 12582912 | tf_op jit(solution)/shard_map/psum | solution.py:31
  485.0 123.0 %copy-start.63 = (pred[2,1024]{1,0:T(4,128)(4,1)}, pred[2,1024]{1,0:T(4,128)(4,1)S(1)}, u32[]{:S(2)}) copy-start(pred[2,1024]{1,0:T(4,128)(4,1)S(1)} %get-tuple-element.563) | copy-start | bytes 6148
  485.1 126.2 %copy-start.58 = (f32[768]{0:T(1024)S(1)}, f32[768]{0:T(1024)}, u32[]{:S(2)}) copy-start(f32[768]{0:T(1024)} %get-tuple-element.455) | copy-start | bytes 9220
  681.5 120.0 %copy-start.51 = (f32[2048]{0:T(1024)S(1)}, f32[2048]{0:T(1024)}, u32[]{:S(2)}) copy-start(f32[2048]{0:T(1024)} %copy-done.50) | copy-start | bytes 24580
  681.5 120.0 %copy-start.59 = (f32[768]{0:T(1024)S(1)}, f32[768]{0:T(1024)}, u32[]{:S(2)}) copy-start(f32[768]{0:T(1024)} %get-tuple-element.455) | copy-start | bytes 9220
  681.5 265.1 %all-reduce.16.cloned.1.call-start = ((), (), s32[]{:S(2)}) async-start(), calls=%async_computation.13 | async-start | bytes 12582912 | tf_op jit(solution)/shard_map/psum | solution.py:31
  801.5 6.4 copy-start.9
  801.5 10.2 slice-start
  811.7 8.6 copy-start.8
  812.2 9.9 copy-start.77
  826.6 120.0 %copy-start.56 = (f32[2048]{0:T(1024)S(1)}, f32[2048]{0:T(1024)}, u32[]{:S(2)}) copy-start(f32[2048]{0:T(1024)} %copy-done.55) | copy-start | bytes 24580
  826.6 120.0 %copy-start.61 = (f32[768]{0:T(1024)S(1)}, f32[768]{0:T(1024)}, u32[]{:S(2)}) copy-start(f32[768]{0:T(1024)} %get-tuple-element.456) | copy-start | bytes 9220
  826.6 320.2 %all-reduce.18.cloned.1.call-start = ((), (), s32[]{:S(2)}) async-start(), calls=%async_computation.14 | async-start | bytes 12582912 | tf_op jit(solution)/shard_map/psum | solution.py:31
  946.6 6.4 copy-start.10
  953.0 8.3 copy-start.21
  965.4 50.7 %copy-start.26 = (f32[2,1024,32]{1,2,0:T(8,128)S(1)}, f32[2,1024,32]{1,2,0:T(8,128)}, u32[]{:S(2)}) copy-start(f32[2,1024,32]{1,2,0:T(8,128)} %copy-done.25) | copy-start | bytes 786436
  971.9 7.2 copy-start.41
  979.0 7.1 copy-start.27
  996.9 7.2 copy-start.41
  1004.1 7.1 copy-start.27
  1026.9 187.9 %reduce-scatter.21.cloned.1.call-start = ((), (), s32[]{:S(2)}) async-start(), calls=%async_computation.19 | async-start | bytes 884736
  1033.0 8.5 copy-start.57
  1033.0 8.4 copy-start.62
  1033.0 252.2 %reduce-scatter.17.cloned.1.call-start = ((), (), s32[]{:S(2)}) async-start(), calls=%async_computation.17 | async-start | bytes 2654208 | tf_op jit(solution)/shard_map/reduce_scatter | solution.py:298
  1041.2 8.3 copy-start.70
  1041.2 8.3 copy-start.71
  1041.2 105.6 %copy-start.47 = (f32[2048]{0:T(1024)S(1)}, f32[2048]{0:T(1024)}, u32[]{:S(2)}) copy-start(f32[2048]{0:T(1024)} %copy-done.46) | copy-start | bytes 24580
  1041.2 105.6 %copy-start.53 = (f32[768]{0:T(1024)S(1)}, f32[768]{0:T(1024)}, u32[]{:S(2)}) copy-start(f32[768]{0:T(1024)} %copy-done.52) | copy-start | bytes 9220
  1041.2 315.8 %reduce-scatter.15.cloned.1.call-start = ((), (), s32[]{:S(2)}) async-start(), calls=%async_computation.16 | async-start | bytes 2654208 | tf_op jit(solution)/shard_map/reduce_scatter | solution.py:297
  1049.4 372.2 %reduce-scatter.23.cloned.1.call-start = ((), (), s32[]{:S(2)}) async-start(), calls=%async_computation.20 | async-start | bytes 442368
  1153.2 7.2 copy-start.69
  1153.2 338.0 %reduce-scatter.13.cloned.1.call-start = ((), (), s32[]{:S(2)}) async-start(), calls=%async_computation.15 | async-start | bytes 2211840 | tf_op jit(solution)/shard_map/reduce_scatter | solution.py:295
  1160.4 451.0 %reduce-scatter.19.cloned.1.call-start = ((), (), s32[]{:S(2)}) async-start(), calls=%async_computation.18 | async-start | bytes 7077888
  1190.8 468.9 %copy-start.73 = (f32[3,96]{1,0:T(4,128)S(1)}, f32[3,96]{1,0:T(4,128)}, u32[]{:S(2)}) copy-start(f32[3,96]{1,0:T(4,128)} %param.43) | copy-start | bytes 3460
  1190.8 468.9 %copy-start.75 = (f32[3,96]{1,0:T(4,128)S(1)}, f32[3,96]{1,0:T(4,128)}, u32[]{:S(2)}) copy-start(f32[3,96]{1,0:T(4,128)} %param.55) | copy-start | bytes 3460
  1190.8 468.9 %copy-start.76 = (f32[3,96]{1,0:T(4,128)S(1)}, f32[3,96]{1,0:T(4,128)}, u32[]{:S(2)}) copy-start(f32[3,96]{1,0:T(4,128)} %param.49) | copy-start | bytes 3460
  1190.8 475.7 %copy-start.32 = (f32[768,96]{0,1:T(8,128)S(1)}, f32[768,96]{0,1:T(8,128)}, u32[]{:S(2)}) copy-start(f32[768,96]{0,1:T(8,128)} %param.42) | copy-start | bytes 884740
  1190.8 478.5 %copy-start.34 = (f32[96,768]{1,0:T(8,128)S(1)}, f32[96,768]{1,0:T(8,128)}, u32[]{:S(2)}) copy-start(f32[96,768]{1,0:T(8,128)} %param.41) | copy-start | bytes 884740
  1190.8 481.3 %copy-start.24 = (f32[2048,96]{0,1:T(8,128)S(1)}, f32[2048,96]{0,1:T(8,128)}, u32[]{:S(2)}) copy-start(f32[2048,96]{0,1:T(8,128)} %param.38) | copy-start | bytes 2359300
  1215.7 395.7 %copy-start.37 = (f32[192,96]{1,0:T(8,128)}, f32[192,96]{1,0:T(8,128)S(1)}, u32[]{:S(2)}) copy-start(f32[192,96]{1,0:T(8,128)S(1)} %copy.139) | copy-start | bytes 221188
  1285.2 381.3 %copy-start.35 = (f32[768,96]{0,1:T(8,128)S(1)}, f32[768,96]{0,1:T(8,128)}, u32[]{:S(2)}) copy-start(f32[768,96]{0,1:T(8,128)} %reduce-scatter.17.cloned.1.call-done) | copy-start | bytes 884740
  1611.4 60.7 %copy-start.23 = (f32[96,2048]{1,0:T(8,128)S(1)}, f32[96,2048]{1,0:T(8,128)}, u32[]{:S(2)}) copy-start(f32[96,2048]{1,0:T(8,128)} %reduce-scatter.19.cloned.1.call-done) | copy-start | bytes 2359300
  1613.8 58.3 %copy-start.38 = (f32[2048,96]{0,1:T(8,128)S(1)}, f32[2048,96]{0,1:T(8,128)}, u32[]{:S(2)}) copy-start(f32[2048,96]{0,1:T(8,128)} %param.50) | copy-start | bytes 2359300
  1659.6 12.5 copy-start.39
  (47 other events, 145.1 us)
Sparse Core Ops, SparseCore 0:
  10.8 63.1 all-gather.7
  91.6 118.1 all-reduce.7
  272.2 119.7 all-reduce.9
  394.6 41.2 all-gather.9
  438.5 39.8 all-gather.11
  484.3 118.3 all-reduce.11
  681.6 119.7 all-reduce.13
  826.7 119.8 all-reduce.15
  1027.0 119.7 all-reduce.17
  1150.5 62.7 reduce-scatter.20
  1217.2 68.0 reduce-scatter.16
  1289.0 67.9 reduce-scatter.14
  1361.2 60.4 reduce-scatter.22
  1425.4 65.8 reduce-scatter.12
  1494.7 116.6 reduce-scatter.18
where the time goes:
time: 1690 us; the launch traced here: 1680 us
  waiting for transfers between devices  1110 us (66%)
  matrix products  170 us (10%)
  blocking collectives  161 us (10%)
  other arithmetic  141 us (8%)
  local copies, waits for them, and re-layouts  69.4 us (4%)
  between operations  25.8 us (2%)
    psum x6, waiting for transfers between devices, tensor_total(): return lax.psum(partial_value, 'tensor')  604 us
    unnamed x18, waiting for transfers between devices  182 us
    reduce_scatter x1, waiting for transfers between devices, per_device(): lax.psum_scatter(upward_grad, 'dp', scatter_dimension=0, tiled=True)  70.1 us
    reduce_scatter x1, waiting for transfers between devices, per_device(): lax.psum_scatter(downward_grad, 'dp', scatter_dimension=1, tiled=True)  68.9 us
    reduce_scatter x1, waiting for transfers between devices, per_device(): lax.psum_scatter(joint_grad, 'dp', scatter_dimension=0, tiled=True)  67.5 us
    all_gather x1, waiting for transfers between devices, per_device(): lax.all_gather(table.astype(jnp.bfloat16), 'dp', axis=1, tiled=True)  62.1 us
    psum x1, blocking collectives, per_device(): square_total = lax.psum(local_square, ('dp', 'tensor'))  39.6 us
    all_gather x1, waiting for transfers between devices, per_device(): lax.all_gather(upward_weight.astype(jnp.bfloat16), 'dp', axis=0, tiled=True)  36 us
  transfers between devices with their start and end apart: 15, of which 14 were waited for; matrix products, arithmetic and copies ran while one was open for 6% of the time, Pallas kernels for 0%

commit v1 on v0

--- a/solution.py
+++ b/solution.py
@@ -2,6 +2,7 @@
 import jax.numpy as jnp
 from jax import lax
 from jax.sharding import PartitionSpec as P
+from jax.lax import axis_index, axis_size, ppermute
 
 D = 768
 HEAD_DIM = 64
@@ -17,6 +18,22 @@
 clip_at = 0.02
 rates = (0.05, 0.03, 0.25, 0.03, 0.03, 0.3)
 decays = (0.1, 0.1, 0.1, 0.1, 0.1, 0.0)
+
+
+def _spread_shifts_all(inner_x, axis_name, out_dim):
+    odd = axis_size(axis_name)
+    field_out = axis_index(axis_name)
+    base_arr, y, mat_out = (odd, field_out, inner_x.shape[out_dim])
+    inter, fresh = (inner_x, 1)
+    while fresh < base_arr:
+        arr_next = ppermute(
+            inter,
+            axis_name=axis_name,
+            perm=[(dev_j, (dev_j - fresh) % base_arr) for dev_j in range(base_arr)],
+        )
+        inter = jnp.concatenate([inter, arr_next], out_dim)
+        fresh = 2 * fresh
+    return jnp.roll(inter, y * mat_out, out_dim)
 
 
 def joined(value, axis, join):
@@ -175,7 +192,7 @@
     variance_gains,
 ):
     vocab_rows, joint_rows, output_rows, upward_rows, downward_rows, gain_rows = (
-        lax.all_gather(table.astype(jnp.bfloat16), "dp", axis=1, tiled=True),
+        _spread_shifts_all(table.astype(jnp.bfloat16), "dp", 1),
         lax.all_gather(joint_weight.astype(jnp.bfloat16), "dp", axis=0, tiled=True),
         lax.all_gather(output_weight.astype(jnp.bfloat16), "dp", axis=1, tiled=True),
         lax.all_gather(upward_weight.astype(jnp.bfloat16), "dp", axis=0, tiled=True),

time: 1690 us -> 1580 us (0.935)
  waiting for transfers between devices: 1110 us -> 974 us
    ppermute x0 -> x3, waiting for transfers between devices: none -> 96.8 us  [_spread_shifts_all(): ppermute(inter, axis_name=axis_name, perm=[(dev_j, (dev_j - fresh) % base...]
    reduce_scatter x1, waiting for transfers between devices: 68.9 us -> 0.01 us  [per_device(): lax.psum_scatter(downward_grad, 'dp', scatter_dimension=1, tiled=True)]
    all_gather x1 -> x0, waiting for transfers between devices: 62.1 us -> none  [per_device(): lax.all_gather(table.astype(jnp.bfloat16), 'dp', axis=1, tiled=True)]
    reduce_scatter x1, waiting for transfers between devices: 70.1 us -> 21.6 us  [per_device(): lax.psum_scatter(upward_grad, 'dp', scatter_dimension=0, tiled=True)]
    all_gather x1, waiting for transfers between devices: 36 us -> 0.03 us  [per_device(): lax.all_gather(upward_weight.astype(jnp.bfloat16), 'dp', axis=0, tiled=True)]
    all_gather x1, waiting for transfers between devices: 23.3 us -> 0.02 us  [per_device(): lax.all_gather(downward_weight.astype(jnp.bfloat16), 'dp', axis=1, tiled=...]
    unnamed x18 -> x17, waiting for transfers between devices: 182 us -> 182 us
  transfers between devices with their start and end apart: 15 -> 17, of which waited for: 14 -> 13; matrix products, arithmetic and copies ran while one was open for 6% -> 7% of each run, Pallas kernels for 0% -> 0%
where the time goes in v1:
time: 1580 us; the launch traced here: 1570 us
  waiting for transfers between devices  974 us (62%)
  matrix products  171 us (11%)
  blocking collectives  165 us (10%)
  other arithmetic  140 us (9%)
  local copies, waits for them, and re-layouts  82.8 us (5%)
  between operations  27.3 us (2%)
    psum x6, waiting for transfers between devices, tensor_total(): return lax.psum(partial_value, 'tensor')  606 us
    unnamed x17, waiting for transfers between devices  182 us
    ppermute x3, waiting for transfers between devices, _spread_shifts_all(): ppermute(inter, axis_name=axis_name, perm=[(dev_j, (dev_j - fresh) % base...  96.8 us
    reduce_scatter x1, waiting for transfers between devices, per_device(): lax.psum_scatter(joint_grad, 'dp', scatter_dimension=0, tiled=True)  67.5 us
    psum x1, blocking collectives, per_device(): square_total = lax.psum(local_square, ('dp', 'tensor'))  39.8 us
    all_gather x1, blocking collectives, per_device(): lax.all_gather(output_weight.astype(jnp.bfloat16), 'dp', axis=1, tiled=True)  33.4 us
    all_gather x1, blocking collectives, per_device(): lax.all_gather(joint_weight.astype(jnp.bfloat16), 'dp', axis=0, tiled=True)  32.5 us
  transfers between devices with their start and end apart: 17, of which 13 were waited for; matrix products, arithmetic and copies ran while one was open for 7% of the time, Pallas kernels for 0%

profile of v1, /device:TPU:0, one launch (start us, length us, event | category | flops | bytes accessed | tf_op | source)
XLA Modules:
  0.0 1570.3 jit_solution(7294664880887900606)
XLA Ops:
  9.5 6.1 collective-permute-start
  15.6 11.2 collective-permute-done
  29.3 17.0 %collective-permute-done.1 = bf16[2048,192]{0,1:T(8,128)(2,1)} collective-permute-done((bf16[2048,192]{0,1:T(8,128)(2,1)S(1)}, bf16[2048,192]{0,1:T(8,128)(2,1)}, u32[]{:S(2)}, u32[]{:S(2)}) %collective-permute-start.1) | collective-permute-done | bytes 786464 | tf_op jit(solution)/shard_map/ppermute | solution.py:29
  50.4 68.7 %collective-permute-done.2 = bf16[2048,384]{1,0:T(8,128)(2,1)} collective-permute-done((bf16[2048,384]{1,0:T(8,128)(2,1)}, bf16[2048,384]{1,0:T(8,128)(2,1)}, u32[]{:S(2)}, u32[]{:S(2)}) %collective-permute-start.2) | collective-permute-done | bytes 1572896 | tf_op jit(solution)/shard_map/ppermute | solution.py:29
  119.0 10.9 concatenate.32
  133.5 9.6 gather_fusion
  143.1 4.6 multiply_select_fusion.1
  148.0 21.6 %all-gather = bf16[8,96,3]{1,2,0:T(4,128)(2,1)S(1)} all-gather(bf16[1,96,3]{1,2,0:T(4,128)(2,1)S(1)} %convert_bitcast_fusion.1), channel_id=1, replica_groups=mesh['dp'=8,'tensor'=4] {'dp'}, dimensions={0}, use_global_device_ids=true | all-gather | bytes 5184 | tf_op jit(solution)/shard_map/all_gather | solution.py:200
  170.7 33.4 %all_gather.26 = bf16[192,768]{0,1:T(8,128)(2,1)} all-gather(bf16[192,96]{0,1:T(8,128)(2,1)S(1)} %copy.134), channel_id=1, replica_groups=mesh['dp'=8,'tensor'=4] {'dp'}, dimensions={1}, use_global_device_ids=true | all-gather | bytes 331776 | tf_op jit(solution)/shard_map/all_gather | solution.py:197
  205.8 32.5 %all_gather.25 = bf16[768,576]{1,0:T(8,128)(2,1)S(1)} all-gather(bf16[96,576]{1,0:T(8,128)(2,1)S(1)} %convert_element_type.106), channel_id=1, replica_groups=mesh['dp'=8,'tensor'=4] {'dp'}, dimensions={0}, use_global_device_ids=true | all-gather | bytes 995328 | tf_op jit(solution)/shard_map/all_gather | solution.py:196
  238.3 31.2 %all-reduce.8.cloned.1.call-done = f32[2048,768]{1,0:T(8,128)} async-done(((f32[2048,768]{1,0:T(8,128)}), f32[2048,768]{1,0:T(8,128)}) %all-reduce.8.cloned.1.call-update) | async-done | bytes 6291472 | tf_op jit(solution)/shard_map/psum | solution.py:48
  274.1 4.5 fusion.113
  278.6 7.5 reshape.255
  295.7 29.3 %while.72 = (s32[]{:T(128)}, bf16[2,1024,3,64]{1,3,2,0:T(8,128)(2,1)}, f32[2,3,1024]{2,1,0:T(4,128)S(1)}, bf16[2,1024,3,64]{1,3,2,0:T(8,128)(2,1)}, s32[2,1024]{...) while((s32[]{:T(128)}, ...), condition=%wide.region_8.9_spmd.clone, body=%wide.region_5.8_spmd.sunk.clone | while | flops 844297216 | bytes 47835256 | solution.py:225
  296.3 4.2 fusion.200
  300.6 3.9 fusion.201
  304.5 5.7 fusion.202
  310.9 4.2 fusion.200
  315.2 3.9 fusion.201
  319.0 5.7 fusion.202
  333.5 118.2 %all-reduce.10.cloned.1.call-done = f32[2048,768]{1,0:T(8,128)} async-done(((f32[2048,768]{1,0:T(8,128)}), f32[2048,768]{1,0:T(8,128)}) %all-reduce.10.cloned.1.call-update) | async-done | bytes 6291472 | tf_op jit(solution)/shard_map/psum | solution.py:48
  451.7 7.9 multiply_reduce_fusion.8
  459.7 19.1 %multiply_convert_fusion.3 = (bf16[2048,768]{1,0:T(8,128)(2,1)S(1)}, f32[2048,768]{1,0:T(8,128)}, f32[2048,768]{1,0:T(8,128)}) fusion(bf16[768,768]{1,0:T(8,128)(2,1)} %all-gather.7.cloned.1.call-done, f32[2048,768]{1,0:T(8,128)} %get-tuple-element.520, f32[768]{0:T(1024)S(1)} %copy-done.61, f32[2048]{0:T(1024)S(1)} %add_rsqrt_fusion.1), kind=kOutput, calls=%fused_computation.111 | convolution fusion | flops 2522873856 | bytes 23211008 | tf_op jit(solution)/shard_map/dot_general | solution.py:232
  478.9 6.7 fusion.125
  486.5 119.1 %all-reduce.12.cloned.1.call-done = f32[2048,768]{1,0:T(8,128)} async-done(((f32[2048,768]{1,0:T(8,128)}), f32[2048,768]{1,0:T(8,128)}) %all-reduce.12.cloned.1.call-update) | async-done | bytes 6291472 | tf_op jit(solution)/shard_map/psum | solution.py:48
  605.6 5.4 multiply_reduce_fusion.7
  616.6 16.7 %while.73 = (s32[]{:T(128)}, f32[2,1024]{1,0:T(2,128)S(1)}, f32[2,1024]{1,0:T(2,128)S(1)}, f32[2,1024]{1,0:T(2,128)S(1)}, bf16[2,1024,768]{2,1,0:T(8,128)(2,1)},...) while((s32[]{:T(128)}, f32[2,1024]{1,0:T(2,128)S(1)}, ...), condition=%wide.region_17.18_spmd.clone, body=%wide.region_13.17_spmd.sunk.clone | while | flops 3233806336 | bytes 21549172 | solution.py:239
  616.6 4.9 fusion.204
  624.9 4.9 fusion.204
  633.3 5.2 all-gather.2
  638.5 5.2 all-gather.1
  643.7 5.2 all-gather.3
  650.3 34.0 %while.76 = (s32[]{:T(128)}, f32[2048,768]{1,0:T(8,128)}, f32[2,1024,768]{2,1,0:T(8,128)}, f32[2,1024]{1,0:T(2,128)S(1)}, bf16[2,1024,768]{2,1,0:T(8,128)(2,1)},...) while((s32[]{:T(128)}, f32[2048,768]{1,0:T(8,128)}, ...), condition=%wide.region_25.26_spmd.clone.clone, body=%wide.region_24.25_spmd.clone.sunk.clone | while | flops 9679406080 | bytes 151032080 | solution.py:259
  650.4 5.7 multiply_convert_fusion.15
  656.1 5.1 select_add_fusion.3
  667.4 5.6 multiply_convert_fusion.15
  673.1 5.1 select_add_fusion.3
  684.4 119.9 %all-reduce.14.cloned.1.call-done = f32[2048,768]{1,0:T(8,128)} async-done(((f32[2048,768]{1,0:T(8,128)}), f32[2048,768]{1,0:T(8,128)}) %all-reduce.14.cloned.1.call-update) | async-done | bytes 6291472 | tf_op jit(solution)/shard_map/psum | solution.py:48
  804.3 6.3 multiply_reduce_fusion.1
  815.0 8.1 add_convert_fusion
  824.9 4.6 fusion.126
  829.6 119.9 %all-reduce.16.cloned.1.call-done = f32[2048,768]{1,0:T(8,128)} async-done(((f32[2048,768]{1,0:T(8,128)}), f32[2048,768]{1,0:T(8,128)}) %all-reduce.16.cloned.1.call-update) | async-done | bytes 6291472 | tf_op jit(solution)/shard_map/psum | solution.py:48
  949.4 6.1 multiply_reduce_fusion.2
  955.9 5.6 multiply_add_fusion.1
  968.2 50.6 %while.75 = (s32[]{:T(128)}, f32[2,1024,3,64]{1,3,2,0:T(8,128)}, f32[2,1024,3,64]{1,3,2,0:T(8,128)}, bf16[2,1024,3,64]{1,3,2,0:T(8,128)(2,1)}, bf16[2,1024,3,64]...) while((s32[]{:T(128)}, f32[2,1024,3,64]{1,3,2,0:T(8,128)}, ...), condition=%wide.region_32.33_spmd.clone, body=%wide.region_30.32_spmd.sunk.clone | while | flops 2061890560 | bytes 135247168 | solution.py:289
  974.7 7.1 multiply_reduce_fusion.18
  981.9 7.1 multiply_convert_fusion.14
  999.7 7.1 multiply_reduce_fusion.18
  1006.9 7.1 multiply_convert_fusion.14
  1025.0 4.7 fusion.127
  1030.8 5.0 fusion.95
  1035.9 8.1 fusion.89
  1044.2 7.9 fusion.110
  1052.3 97.3 %all-reduce.18.cloned.1.call-done = f32[2048,768]{1,0:T(8,128)} async-done(((f32[2048,768]{1,0:T(8,128)}), f32[2048,768]{1,0:T(8,128)}) %all-reduce.18.cloned.1.call-update) | async-done | bytes 6291472 | tf_op jit(solution)/shard_map/psum | solution.py:48
  1149.6 5.4 multiply_reduce_fusion.3
  1156.1 7.1 fusion.112
  1163.3 23.8 %scatter_custom_fusion = f32[2048,768]{1,0:T(8,128)} fusion(f32[2048,768]{1,0:T(8,128)} %get-tuple-element.250, s32[2048]{0:T(1024)} %copy-done.66, f32[2048,768]{1,0:T(8,128)} %copy-done.5, f32[2048,768]{1,0:T(8,128)} %all-reduce.18.cloned.1.call-done, f32[2048,768]{1,0:T(8,128)} %all-reduce.8.cloned.1.call-done, f32[2048]{0:T(1024)S(1)} %broadcast_multiply_fusion, ...), kind=kCustom, calls=%fused_computation.95 | custom fusion | flops 15728640 | bytes 25188352 | tf_op jit(solution)/shard_map/scatter-add | solution.py:307
  1187.1 6.6 copy.142
  1195.3 21.9 %all-reduce = (f32[]{:T(128)}, f32[]{:T(128)}) all-reduce(f32[]{:T(128)} %get-tuple-element.513, f32[]{:T(128)} %convert_reduce_fusion.1), channel_id=1, replica_groups=mesh['dp'=8,'tensor'=4] {'dp'}, use_global_device_ids=true, to_apply=%region_21.22 | all-reduce | flops 2 | bytes 16 | tf_op jit(solution)/shard_map/psum | solution.py:250
  1221.2 21.6 %reduce-scatter.15.cloned.1.call-done = f32[96,768]{1,0:T(8,128)} async-done(((f32[768,768]{1,0:T(8,128)}), f32[96,768]{1,0:T(8,128)}) %reduce-scatter.15.cloned.1.call-update) | async-done | bytes 294928 | tf_op jit(solution)/shard_map/reduce_scatter | solution.py:314
  1244.5 63.2 %reduce-scatter.23.cloned.1.call-done = f32[96,3]{1,0:T(8,128)} async-done(((f32[768,3]{1,0:T(8,128)}), f32[96,3]{1,0:T(8,128)}) %reduce-scatter.23.cloned.1.call-update) | async-done | bytes 1168
  1309.8 67.5 %reduce-scatter.13.cloned.1.call-done = f32[96,576]{1,0:T(8,128)} async-done(((f32[768,576]{1,0:T(8,128)}), f32[96,576]{1,0:T(8,128)}) %reduce-scatter.13.cloned.1.call-update) | async-done | bytes 221200 | tf_op jit(solution)/shard_map/reduce_scatter | solution.py:312
  1378.9 118.6 %reduce-scatter.19.cloned.1.call-done = f32[96,2048]{1,0:T(8,128)} async-done(((f32[768,2048]{1,0:T(8,128)}), f32[96,2048]{1,0:T(8,128)}) %reduce-scatter.19.cloned.1.call-update) | async-done | bytes 786448
  1504.5 39.8 %psum.71 = f32[]{:T(128)} all-reduce(f32[]{:T(128)S(6)} %add.267), channel_id=1, replica_groups=mesh['dp'=8,'tensor'=4] {'dp','tensor'}, use_global_device_ids=true, to_apply=%region_51.52 | all-reduce | flops 1 | bytes 8 | tf_op jit(solution)/shard_map/psum | solution.py:323
  (382 shorter events, 134.4 us)
Async XLA Ops:
  8.0 42.2 %copy-start.54 = (s32[2048]{0:T(1024)S(1)}, s32[2048]{0:T(1024)}, u32[]{:S(2)}) copy-start(s32[2048]{0:T(1024)} %param.33) | copy-start | bytes 24580
  8.0 42.2 %copy-start.73 = (s32[2048]{0:T(1024)S(1)}, s32[2048]{0:T(1024)}, u32[]{:S(2)}) copy-start(s32[2048]{0:T(1024)} %param.36) | copy-start | bytes 24580
  8.0 261.4 %all-reduce.8.cloned.1.call-start = ((), (), s32[]{:S(2)}) async-start(), calls=%async_computation.6 | async-start | bytes 12582912 | tf_op jit(solution)/shard_map/psum | solution.py:48
  9.5 17.2 %collective-permute-start = (bf16[2048,96]{1,0:T(8,128)(2,1)S(1)}, bf16[2048,96]{1,0:T(8,128)(2,1)S(1)}, u32[]{:S(2)}, u32[]{:S(2)}) collective-permute-start(bf16[2048,96]{1,0:T(8,128)(2,1)S(1)} %copy.124), channel_id=1, source_target_pairs={{0,28},{4,0},{8,4},{12,8},{16,12},{20,16},{24,20},{28,24},{1,29},{... | collective-permute-start | bytes 1179656 | tf_op jit(solution)/shard_map/ppermute | solution.py:29
  27.7 18.6 %collective-permute-start.1 = (bf16[2048,192]{0,1:T(8,128)(2,1)S(1)}, bf16[2048,192]{0,1:T(8,128)(2,1)}, u32[]{:S(2)}, u32[]{:S(2)}) collective-permute-start(bf16[2048,192]{0,1:T(8,128)(2,1)S(1)} %copy.125), channel_id=1, source_target_pairs={{0,24},{4,28},{8,0},{12,4},{16,8},{20,12},{24,16},{28,20},{1,25},{... | collective-permute-start | bytes 2359304 | tf_op jit(solution)/shard_map/ppermute | solution.py:29
  49.8 69.3 %collective-permute-start.2 = (bf16[2048,384]{1,0:T(8,128)(2,1)}, bf16[2048,384]{1,0:T(8,128)(2,1)}, u32[]{:S(2)}, u32[]{:S(2)}) collective-permute-start(bf16[2048,384]{1,0:T(8,128)(2,1)} %pad_maximum_fusion.1), channel_id=1, source_target_pairs={{0,16},{4,20},{8,24},{12,28},{16,0},{20,4},{24,8},{28,12},{1,17},{... | collective-permute-start | bytes 4718600 | tf_op jit(solution)/shard_map/ppermute | solution.py:29
  50.3 68.7 %copy-start.67 = (pred[2048]{0:T(1024)(128)(4,1)}, pred[2048]{0:T(1024)(128)(4,1)S(1)}, u32[]{:S(2)}) copy-start(pred[2048]{0:T(1024)(128)(4,1)S(1)} %get-tuple-element.522) | copy-start | bytes 6148
  50.3 92.7 %copy-start.69 = (pred[2048]{0:T(1024)(128)(4,1)}, pred[2048]{0:T(1024)(128)(4,1)S(1)}, u32[]{:S(2)}) copy-start(pred[2048]{0:T(1024)(128)(4,1)S(1)} %get-tuple-element.521) | copy-start | bytes 6148
  50.3 68.7 %copy-start.66 = (s32[2048]{0:T(1024)}, s32[2048]{0:T(1024)S(1)}, u32[]{:S(2)}) copy-start(s32[2048]{0:T(1024)S(1)} %get-tuple-element.524) | copy-start | bytes 24580
  133.4 9.6 copy-start
  143.1 26.6 %copy-start.45 = (f32[192,96]{1,0:T(8,128)S(1)}, f32[192,96]{1,0:T(8,128)}, u32[]{:S(2)}) copy-start(f32[192,96]{1,0:T(8,128)} %param.40) | copy-start | bytes 221188
  143.1 26.7 %copy-start.36 = (f32[96,576]{1,0:T(8,128)S(1)}, f32[96,576]{1,0:T(8,128)}, u32[]{:S(2)}) copy-start(f32[96,576]{1,0:T(8,128)} %param.39) | copy-start | bytes 663556
  147.7 304.0 %all-reduce.10.cloned.1.call-start = ((), (), s32[]{:S(2)}) async-start(), calls=%async_computation.7 | async-start | bytes 12582912 | tf_op jit(solution)/shard_map/psum | solution.py:48
  170.6 108.1 %copy-start.52 = (f32[768]{0:T(1024)}, f32[768]{0:T(1024)S(1)}, u32[]{:S(2)}) copy-start(f32[768]{0:T(1024)S(1)} %get-tuple-element.406) | copy-start | bytes 9220
  205.8 87.5 %copy-start.25 = (f32[2,1024,32]{1,2,0:T(8,128)}, f32[2,1024,32]{1,2,0:T(8,128)S(1)}, u32[]{:S(2)}) copy-start(f32[2,1024,32]{1,2,0:T(8,128)S(1)} %get-tuple-element.551) | copy-start | bytes 786436
  238.3 40.3 %copy-start.18 = (bf16[768,576]{1,0:T(8,128)(2,1)}, bf16[768,576]{1,0:T(8,128)(2,1)S(1)}, u32[]{:S(2)}) copy-start(bf16[768,576]{1,0:T(8,128)(2,1)S(1)} %all_gather.25) | copy-start | bytes 2654212
  295.7 32.4 %copy-start.20 = (bf16[192,768]{0,1:T(8,128)(2,1)S(1)}, bf16[192,768]{0,1:T(8,128)(2,1)}, u32[]{:S(2)}) copy-start(bf16[192,768]{0,1:T(8,128)(2,1)} %all_gather.26) | copy-start | bytes 884740
  325.0 161.4 %copy-start.43 = (s32[2,1024]{1,0:T(2,128)}, s32[2,1024]{1,0:T(2,128)S(1)}, u32[]{:S(2)}) copy-start(s32[2,1024]{1,0:T(2,128)S(1)} %get-tuple-element.1126) | copy-start | bytes 24580
  331.8 127.9 %all-gather.7.cloned.1.call-start = ((), (), s32[]{:S(2)}) async-start(), calls=%async_computation.8 | async-start | bytes 1327104 | tf_op jit(solution)/shard_map/all_gather | solution.py:198
  332.5 146.3 %all-gather.9.cloned.1.call-start = ((), (), s32[]{:S(2)}) async-start(), calls=%async_computation.9 | async-start | bytes 1327104 | tf_op jit(solution)/shard_map/all_gather | solution.py:199
  333.4 126.3 %copy-start.61 = (f32[768]{0:T(1024)S(1)}, f32[768]{0:T(1024)}, u32[]{:S(2)}) copy-start(f32[768]{0:T(1024)} %get-tuple-element.405) | copy-start | bytes 9220
  333.4 272.2 %all-reduce.12.cloned.1.call-start = ((), (), s32[]{:S(2)}) async-start(), calls=%async_computation.10 | async-start | bytes 12582912 | tf_op jit(solution)/shard_map/psum | solution.py:48
  459.7 19.2 %copy-start.56 = (f32[2048]{0:T(1024)}, f32[2048]{0:T(1024)S(1)}, u32[]{:S(2)}) copy-start(f32[2048]{0:T(1024)S(1)} %add_rsqrt_fusion.1) | copy-start | bytes 24580
  485.6 318.7 %all-reduce.14.cloned.1.call-start = ((), (), s32[]{:S(2)}) async-start(), calls=%async_computation.11 | async-start | bytes 12582912 | tf_op jit(solution)/shard_map/psum | solution.py:48
  486.5 124.5 %copy-start.64 = (pred[2,1024]{1,0:T(4,128)(4,1)}, pred[2,1024]{1,0:T(4,128)(4,1)S(1)}, u32[]{:S(2)}) copy-start(pred[2,1024]{1,0:T(4,128)(4,1)S(1)} %get-tuple-element.512) | copy-start | bytes 6148
  486.5 127.7 %copy-start.59 = (f32[768]{0:T(1024)S(1)}, f32[768]{0:T(1024)}, u32[]{:S(2)}) copy-start(f32[768]{0:T(1024)} %get-tuple-element.404) | copy-start | bytes 9220
  684.3 120.0 %copy-start.51 = (f32[2048]{0:T(1024)S(1)}, f32[2048]{0:T(1024)}, u32[]{:S(2)}) copy-start(f32[2048]{0:T(1024)} %copy-done.50) | copy-start | bytes 24580
  684.3 120.0 %copy-start.60 = (f32[768]{0:T(1024)S(1)}, f32[768]{0:T(1024)}, u32[]{:S(2)}) copy-start(f32[768]{0:T(1024)} %get-tuple-element.404) | copy-start | bytes 9220
  684.4 265.1 %all-reduce.16.cloned.1.call-start = ((), (), s32[]{:S(2)}) async-start(), calls=%async_computation.12 | async-start | bytes 12582912 | tf_op jit(solution)/shard_map/psum | solution.py:48
  804.3 10.2 slice-start
  814.6 8.6 copy-start.8
  815.0 9.9 copy-start.79
  829.5 120.0 %copy-start.57 = (f32[2048]{0:T(1024)S(1)}, f32[2048]{0:T(1024)}, u32[]{:S(2)}) copy-start(f32[2048]{0:T(1024)} %copy-done.56) | copy-start | bytes 24580
  829.5 120.0 %copy-start.62 = (f32[768]{0:T(1024)S(1)}, f32[768]{0:T(1024)}, u32[]{:S(2)}) copy-start(f32[768]{0:T(1024)} %get-tuple-element.405) | copy-start | bytes 9220
  829.5 320.1 %all-reduce.18.cloned.1.call-start = ((), (), s32[]{:S(2)}) async-start(), calls=%async_computation.13 | async-start | bytes 12582912 | tf_op jit(solution)/shard_map/psum | solution.py:48
  955.9 8.2 copy-start.21
  968.2 50.7 %copy-start.26 = (f32[2,1024,32]{1,2,0:T(8,128)S(1)}, f32[2,1024,32]{1,2,0:T(8,128)}, u32[]{:S(2)}) copy-start(f32[2,1024,32]{1,2,0:T(8,128)} %copy-done.25) | copy-start | bytes 786436
  974.7 7.2 copy-start.41
  981.9 7.1 copy-start.27
  999.7 7.2 copy-start.41
  1029.6 188.2 %reduce-scatter.21.cloned.1.call-start = ((), (), s32[]{:S(2)}) async-start(), calls=%async_computation.18 | async-start | bytes 884736
  1035.8 8.4 copy-start.58
  1035.8 8.4 copy-start.63
  1035.8 183.7 %reduce-scatter.17.cloned.1.call-start = ((), (), s32[]{:S(2)}) async-start(), calls=%async_computation.16 | async-start | bytes 2654208 | tf_op jit(solution)/shard_map/reduce_scatter | solution.py:315
  1044.0 8.3 copy-start.71
  1044.0 8.3 copy-start.72
  1044.0 105.7 %copy-start.47 = (f32[2048]{0:T(1024)S(1)}, f32[2048]{0:T(1024)}, u32[]{:S(2)}) copy-start(f32[2048]{0:T(1024)} %copy-done.46) | copy-start | bytes 24580
  1044.0 105.7 %copy-start.53 = (f32[768]{0:T(1024)S(1)}, f32[768]{0:T(1024)}, u32[]{:S(2)}) copy-start(f32[768]{0:T(1024)} %copy-done.52) | copy-start | bytes 9220
  1044.0 198.8 %reduce-scatter.15.cloned.1.call-start = ((), (), s32[]{:S(2)}) async-start(), calls=%async_computation.15 | async-start | bytes 2654208 | tf_op jit(solution)/shard_map/reduce_scatter | solution.py:314
  1052.2 255.5 %reduce-scatter.23.cloned.1.call-start = ((), (), s32[]{:S(2)}) async-start(), calls=%async_computation.19 | async-start | bytes 442368
  1156.1 7.2 copy-start.70
  1156.1 221.2 %reduce-scatter.13.cloned.1.call-start = ((), (), s32[]{:S(2)}) async-start(), calls=%async_computation.14 | async-start | bytes 2211840 | tf_op jit(solution)/shard_map/reduce_scatter | solution.py:312
  1163.2 334.3 %reduce-scatter.19.cloned.1.call-start = ((), (), s32[]{:S(2)}) async-start(), calls=%async_computation.17 | async-start | bytes 7077888
  1193.7 352.0 %copy-start.75 = (f32[3,96]{1,0:T(4,128)S(1)}, f32[3,96]{1,0:T(4,128)}, u32[]{:S(2)}) copy-start(f32[3,96]{1,0:T(4,128)} %param.43) | copy-start | bytes 3460
  1193.7 352.0 %copy-start.77 = (f32[3,96]{1,0:T(4,128)S(1)}, f32[3,96]{1,0:T(4,128)}, u32[]{:S(2)}) copy-start(f32[3,96]{1,0:T(4,128)} %param.55) | copy-start | bytes 3460
  1193.7 352.0 %copy-start.78 = (f32[3,96]{1,0:T(4,128)S(1)}, f32[3,96]{1,0:T(4,128)}, u32[]{:S(2)}) copy-start(f32[3,96]{1,0:T(4,128)} %param.49) | copy-start | bytes 3460
  1193.7 358.6 %copy-start.32 = (f32[768,96]{0,1:T(8,128)S(1)}, f32[768,96]{0,1:T(8,128)}, u32[]{:S(2)}) copy-start(f32[768,96]{0,1:T(8,128)} %param.42) | copy-start | bytes 884740
  1193.8 361.4 %copy-start.34 = (f32[96,768]{1,0:T(8,128)S(1)}, f32[96,768]{1,0:T(8,128)}, u32[]{:S(2)}) copy-start(f32[96,768]{1,0:T(8,128)} %param.41) | copy-start | bytes 884740
  1193.8 364.1 %copy-start.24 = (f32[2048,96]{0,1:T(8,128)S(1)}, f32[2048,96]{0,1:T(8,128)}, u32[]{:S(2)}) copy-start(f32[2048,96]{0,1:T(8,128)} %param.38) | copy-start | bytes 2359300
  1218.9 278.6 %copy-start.37 = (f32[192,96]{1,0:T(8,128)}, f32[192,96]{1,0:T(8,128)S(1)}, u32[]{:S(2)}) copy-start(f32[192,96]{1,0:T(8,128)S(1)} %copy.145) | copy-start | bytes 221188
  1219.5 332.9 %copy-start.35 = (f32[768,96]{0,1:T(8,128)S(1)}, f32[768,96]{0,1:T(8,128)}, u32[]{:S(2)}) copy-start(f32[768,96]{0,1:T(8,128)} %reduce-scatter.17.cloned.1.call-done) | copy-start | bytes 884740
  1497.5 60.4 %copy-start.23 = (f32[96,2048]{1,0:T(8,128)S(1)}, f32[96,2048]{1,0:T(8,128)}, u32[]{:S(2)}) copy-start(f32[96,2048]{1,0:T(8,128)} %reduce-scatter.19.cloned.1.call-done) | copy-start | bytes 2359300
  1499.9 58.0 %copy-start.38 = (f32[2048,96]{0,1:T(8,128)S(1)}, f32[2048,96]{0,1:T(8,128)}, u32[]{:S(2)}) copy-start(f32[2048,96]{0,1:T(8,128)} %param.50) | copy-start | bytes 2359300
  1545.7 12.2 copy-start.39
  (51 other events, 183.1 us)
Sparse Core Ops, SparseCore 0:
  147.9 121.5 all-reduce.7
  331.9 119.7 all-reduce.9
  485.8 119.7 all-reduce.11
  684.5 119.7 all-reduce.13
  829.6 119.7 all-reduce.15
  1029.8 119.8 all-reduce.17
Sparse Core Ops, SparseCore 1:
  335.0 41.6 all-gather.6
  379.3 40.0 all-gather.8
  1035.9 62.9 reduce-scatter.20
  1102.7 68.0 reduce-scatter.16
  1174.7 68.0 reduce-scatter.14
  1247.0 60.6 reduce-scatter.22
  1311.4 65.8 reduce-scatter.12
  1380.7 116.7 reduce-scatter.18
